TPU v7x, 128 devices: a whole 4x4x4 slice. The times are simulated.
128 devices in a mesh: row: 8 (over x_hi, z), rep: 16 (over x_lo, y, core).
Axes of the slice: x: 4 (x_hi: 2, x_lo: 2; x = x_hi * 2 + x_lo), y: 4, z: 4, core: 2. Of those that a mesh axis runs over, the one named last changes fastest.
Arguments:
- features: bfloat16 [32768, 256], P('row'), may hold values from 0 to 2
- self_weight: bfloat16 [256, 256], replicated, may hold values from -0.375 to 0.375
- neigh_weight: bfloat16 [256, 256], replicated, may hold values from -0.375 to 0.375
- out_bias: float32 [256], replicated, may hold values from -4 to 4
- tile_masks: int32 [32768, 128, 128], P('row', 'rep'), may hold values 0 or 1
- tile_live: int32 [256, 128], P('row', 'rep'), may hold values from 0 to 1, as said below
- tile_columns: int32 [256, 128], P('row', 'rep'), may hold values from 0 to 1
- node_degree: int32 [32768], P(('row', 'rep')), may hold values from 128 to 511
- cotangent: bfloat16 [32768, 256], P(('row', 'rep')), may hold values from -6 to 6
Outputs:
- hidden_out: bfloat16 [32768, 256], P(('row', 'rep'))
- grad_features: bfloat16 [32768, 256], P(('row', 'rep'))
- grad_self: float32 [256, 256], replicated
- grad_neigh: float32 [256, 256], replicated
- grad_bias: float32 [256], replicated
Inputs may be any that keep to these rules, and one draw needn't show every extreme that they name: `tile_masks`: an edge bit; bits of slots without a tile are not read. `tile_live`: 1 where the slot holds a tile. `tile_columns`: the covered block among the 2 blocks of that column set and panel.
All inputs are finite; a program needn't handle non-finite values. No bound on the sum of `tile_masks` on one device may be relied on, other than what follows from the above.
Results may differ from a plain program's by a relative error of at most 0.0053.
Values may be sent and summed in bfloat16 or wider, within the bound.
A program may use at most 128 MiB of HBM per device.

v0:
```python
import math
import jax
import jax.numpy as jnp
from jax import lax
from jax.sharding import PartitionSpec as P


def activation(values):
    return jax.nn.gelu(values, approximate=True)


def per_device(
    features,
    self_weight,
    neigh_weight,
    out_bias,
    tile_masks,
    tile_live,
    tile_columns,
    node_degree,
    cotangent,
):
    row_devices = lax.axis_size("row")
    rep_devices = lax.axis_size("rep")
    panel_rows, width = features.shape
    share_rows = node_degree.shape[0]
    panel_count = tile_masks.shape[1]
    tile_size = tile_masks.shape[2]
    block_rows = panel_rows // tile_size
    set_blocks = share_rows // tile_size
    column_rows = panel_count * share_rows
    contract_first = (((0,), (0,)), ((), ()))
    contract_second = (((1,), (1,)), ((), ()))
    block_ids = jnp.arange(set_blocks, dtype=jnp.int32)
    selected = (tile_columns[:, :, None] == block_ids[None, None, :]) & (tile_live[:, :, None] != 0)
    keeper = selected.astype(jnp.bfloat16)
    dense = tile_masks.reshape(block_rows, tile_size, panel_count, 1, tile_size).astype(
        jnp.bfloat16
    )
    dense = (dense * keeper[:, None, :, :, None]).reshape(panel_rows, column_rows)
    own = lax.dynamic_slice_in_dim(features, lax.axis_index("rep") * share_rows, share_rows, 0)
    strip = dense
    partial_sums = jnp.dot(
        strip, lax.all_gather(own, "row", axis=0, tiled=True), preferred_element_type=jnp.float32
    )
    agg_sum = lax.psum_scatter(partial_sums, "rep", scatter_dimension=0, tiled=True)
    degree = node_degree.astype(jnp.float32)[:, None]
    mean = (agg_sum / degree).astype(jnp.bfloat16)
    pre = (
        jnp.dot(own, self_weight, preferred_element_type=jnp.float32)
        + jnp.dot(mean, neigh_weight, preferred_element_type=jnp.float32)
        + out_bias
    )
    result, pull = jax.vjp(activation, pre)
    hidden_out = result.astype(jnp.bfloat16)
    dpre = pull(cotangent.astype(jnp.float32))[0]
    dpre_b = dpre.astype(jnp.bfloat16)
    scale = 1.0 / math.sqrt(share_rows * row_devices * rep_devices)
    self_term = (
        lax.dot_general(own, dpre_b, contract_first, preferred_element_type=jnp.float32) * scale
    )
    neigh_term = (
        lax.dot_general(mean, dpre_b, contract_first, preferred_element_type=jnp.float32) * scale
    )
    bias_term = jnp.sum(dpre, axis=0) * scale
    grad_self, grad_neigh, grad_bias = lax.psum((self_term, neigh_term, bias_term), ("row", "rep"))
    message = (
        lax.dot_general(dpre_b, neigh_weight, contract_second, preferred_element_type=jnp.float32)
        / degree
    ).astype(jnp.bfloat16)
    direct = lax.dot_general(
        dpre_b, self_weight, contract_second, preferred_element_type=jnp.float32
    )
    strip = dense
    partial_back = lax.dot_general(
        strip,
        lax.all_gather(message, "rep", axis=0, tiled=True),
        contract_first,
        preferred_element_type=jnp.float32,
    )
    spread = lax.psum_scatter(
        partial_back.astype(jnp.bfloat16), "row", scatter_dimension=0, tiled=True
    ).astype(jnp.float32)
    grad_features = (direct + spread).astype(jnp.bfloat16)
    return (hidden_out, grad_features, grad_self, grad_neigh, grad_bias)


def solution(mesh):
    return jax.shard_map(
        per_device,
        mesh=mesh,
        in_specs=(
            P("row", None),
            P(),
            P(),
            P(),
            P("row", "rep", None),
            P("row", "rep"),
            P("row", "rep"),
            P(("row", "rep")),
            P(("row", "rep"), None),
        ),
        out_specs=(P(("row", "rep"), None), P(("row", "rep"), None), P(), P(), P()),
        check_vma=False,
    )
```

profile of v0, /device:TPU:1, one launch (start us, length us, event | category | flops | bytes accessed | tf_op | source)
XLA Modules:
  0.0 428.5 jit_solution(4350122207436884132)
XLA Ops:
  7.2 1.5 copy-done
  8.8 0.7 constant_dynamic-slice_fusion
  9.5 0.8 copy.14
  10.3 0.7 broadcast_compare_fusion
  11.1 6.3 %convert_element_type.45 = bf16[4096,8,128]{2,1,0:T(8,128)(2,1)S(1)} convert(s32[4096,8,128]{2,1,0:T(8,128)} %param.13) | non-fusion elementwise | flops 4194304 | bytes 25165824 | tf_op jit(solution)/shard_map/convert_element_type | solution.py:37
  17.4 0.1 fusion.13
  17.5 19.8 %broadcast_multiply_fusion = bf16[32,128,8,2,128]{4,3,2,1,0:T(2,128)(2,1)} fusion(bf16[32,8,2]{2,1,0:T(8,128)(2,1)S(1)} %fusion.13, bf16[32,128,8,128]{3,2,1,0:T(8,128)(2,1)S(1)} %bitcast.15), kind=kLoop, calls=%fused_computation | loop fusion | flops 8388608 | bytes 25166848 | tf_op jit(solution)/shard_map/mul | solution.py:40
  37.3 27.8 %mul.80 = bf16[4096,2048]{1,0:T(8,128)(2,1)} reshape(bf16[32,128,8,2,128]{4,3,2,1,0:T(2,128)(2,1)} %broadcast_multiply_fusion) | data formatting | bytes 33554432 | tf_op jit(solution)/shard_map/mul | solution.py:40
  65.2 12.6 %fusion.17 = f32[4096,256]{1,0:T(8,128)} fusion(bf16[4096,2048]{1,0:T(8,128)(2,1)} %mul.80, bf16[2048,256]{1,0:T(8,128)(2,1)} %all-gather.3.cloned.1.call-done), kind=kOutput, calls=%fused_computation.33 | convolution fusion | flops 4294967296 | bytes 22020096 | tf_op jit(solution)/shard_map/dot_general | solution.py:43
  77.9 0.2 fusion.16
  78.1 66.0 %reduce-scatter.3.cloned.1.call-done = f32[256,256]{1,0:T(8,128)} async-done(((f32[4096,256]{1,0:T(8,128)}), f32[256,256]{1,0:T(8,128)}) %reduce-scatter.3.cloned.1.call-update) | async-done | bytes 262160 | tf_op jit(solution)/shard_map/reduce_scatter | solution.py:46
  144.1 2.0 fusion.14
  146.1 0.9 fusion.2
  147.0 0.2 reduce-scatter.5.cloned.1.call-start
  147.3 36.9 %all-gather.5.cloned.1.call-done = bf16[4096,256]{1,0:T(8,128)(2,1)} async-done(((bf16[256,256]{1,0:T(8,128)(2,1)}), bf16[4096,256]{1,0:T(8,128)(2,1)}) %all-gather.5.cloned.1.call-update) | async-done | bytes 2097168 | tf_op jit(solution)/shard_map/all_gather | solution.py:77
  184.1 12.3 %convolution_convert_fusion = bf16[2048,256]{1,0:T(8,128)(2,1)} fusion(bf16[4096,2048]{1,0:T(8,128)(2,1)} %mul.80, bf16[4096,256]{1,0:T(8,128)(2,1)} %all-gather.5.cloned.1.call-done), kind=kOutput, calls=%fused_computation.1 | convolution fusion | flops 4295491584 | bytes 19922944 | tf_op jit(solution)/shard_map/dot_general | solution.py:75
  196.5 0.9 convolution_multiply_fusion.1
  197.4 1.0 convolution_multiply_fusion
  198.5 66.0 %psum.23 = f32[256]{0:T(256)} all-reduce(f32[256]{0:T(256)S(1)} %broadcast_multiply_fusion.1), channel_id=1, replica_groups=mesh['row'=8,'rep'=16] {'row','rep'}, use_global_device_ids=true, to_apply=%region_5.0 | all-reduce | flops 256 | bytes 2048 | tf_op jit(solution)/shard_map/psum | solution.py:66
  264.4 1.8 reduce-scatter.5.cloned.1.call-done
  266.2 1.8 fusion.1
  268.0 150.7 %all-reduce.3.cloned.1.call-done = (f32[256,256]{1,0:T(8,128)}, f32[256,256]{1,0:T(8,128)}) async-done(((f32[256,256]{1,0:T(8,128)}, f32[256,256]{1,0:T(8,128)}), (f32[256,256]{1,0:T(8,128)}, f32[256,256]{1,0:T(8,128)})) %all-reduce.3.cloned.1.call-update) | async-done | bytes 524304 | tf_op jit(solution)/shard_map/psum | solution.py:66
  418.6 1.7 copy.18
  420.3 1.7 copy.19
  (30 shorter events, 0.4 us)
Async XLA Ops:
  7.2 1.6 copy-start
  7.2 58.0 %all-gather.3.cloned.1.call-start = ((), (), s32[]{:S(2)}) async-start(), calls=%async_computation.2 | async-start | bytes 1179648 | tf_op jit(solution)/shard_map/all_gather | solution.py:44
  9.5 134.6 %reduce-scatter.3.cloned.1.call-start = ((), (), s32[]{:S(2)}) async-start(), calls=%async_computation.3 | async-start | bytes 4456448 | tf_op jit(solution)/shard_map/reduce_scatter | solution.py:46
  65.1 12.7 %copy-start.4 = (s32[256]{0:T(256)S(1)}, s32[256]{0:T(256)}, u32[]{:S(2)}) copy-start(s32[256]{0:T(256)} %param.16) | copy-start | bytes 3076
  65.1 12.8 %copy-start.2 = (bf16[256,256]{1,0:T(8,128)(2,1)S(1)}, bf16[256,256]{1,0:T(8,128)(2,1)}, u32[]{:S(2)}) copy-start(bf16[256,256]{1,0:T(8,128)(2,1)} %constant_dynamic-slice_fusion) | copy-start | bytes 393220
  65.1 12.8 %copy-start.3 = (bf16[256,256]{1,0:T(8,128)(2,1)S(1)}, bf16[256,256]{1,0:T(8,128)(2,1)}, u32[]{:S(2)}) copy-start(bf16[256,256]{1,0:T(8,128)(2,1)} %param.10) | copy-start | bytes 393220
  65.1 79.0 %copy-start.6 = (bf16[256,256]{1,0:T(8,128)(2,1)S(1)}, bf16[256,256]{1,0:T(8,128)(2,1)}, u32[]{:S(2)}) copy-start(bf16[256,256]{1,0:T(8,128)(2,1)} %param.17) | copy-start | bytes 393220
  65.1 78.9 %copy-start.7 = (bf16[256,256]{1,0:T(8,128)(2,1)S(1)}, bf16[256,256]{1,0:T(8,128)(2,1)}, u32[]{:S(2)}) copy-start(bf16[256,256]{1,0:T(8,128)(2,1)} %param.11) | copy-start | bytes 393220
  65.1 78.9 %copy-start.8 = (f32[256]{0:T(256)S(1)}, f32[256]{0:T(256)}, u32[]{:S(2)}) copy-start(f32[256]{0:T(256)} %param.12) | copy-start | bytes 3076
  77.8 106.3 %all-gather.5.cloned.1.call-start = ((), (), s32[]{:S(2)}) async-start(), calls=%async_computation.4 | async-start | bytes 2228224 | tf_op jit(solution)/shard_map/all_gather | solution.py:77
  147.0 50.4 %copy-start.5 = (f32[256,256]{1,0:T(8,128)S(1)}, f32[256,256]{1,0:T(8,128)}, u32[]{:S(2)}) copy-start(f32[256,256]{1,0:T(8,128)} %reduce-scatter.3.cloned.1.call-done) | copy-start | bytes 786436
  147.0 274.9 %copy-start.1 = (bf16[4096,256]{1,0:T(8,128)(2,1)S(1)}, bf16[4096,256]{1,0:T(8,128)(2,1)}, u32[]{:S(2)}) copy-start(bf16[4096,256]{1,0:T(8,128)(2,1)} %param.9) | copy-start | bytes 6291460
  147.0 119.2 %reduce-scatter.5.cloned.1.call-start = ((), (), s32[]{:S(2)}) async-start(), calls=%async_computation.5 | async-start | bytes 1179648 | tf_op jit(solution)/shard_map/reduce_scatter | solution.py:81
  196.4 222.2 %all-reduce.3.cloned.1.call-start = ((), (), s32[]{:S(2)}) async-start(), calls=%async_computation.6 | async-start | bytes 1048576 | tf_op jit(solution)/shard_map/psum | solution.py:66
Sparse Core Ops, SparseCore 0:
  11.0 48.4 all-gather.2
  77.9 66.0 reduce-scatter.2
  147.1 36.9 all-gather.4
  196.6 69.5 reduce-scatter.4
  272.3 146.2 all-reduce.2
where the time goes:
time: 430 us; the launch traced here: 429 us
  waiting for transfers between devices  255 us (59%)
  blocking collectives  66 us (15%)
  local copies, waits for them, and re-layouts  34.2 us (8%)
  matrix products  31.7 us (7%)
  other arithmetic  27 us (6%)
  between operations  13.9 us (3%)
    psum x1, waiting for transfers between devices, per_device(): lax.psum((self_term, neigh_term, bias_term), ('row', 'rep'))  151 us
    reduce_scatter x1, waiting for transfers between devices, per_device(): lax.psum_scatter(partial_sums, 'rep', scatter_dimension=0, tiled=True)  66 us
    psum x1, blocking collectives, per_device(): lax.psum((self_term, neigh_term, bias_term), ('row', 'rep'))  66 us
    all_gather x1, waiting for transfers between devices, per_device(): lax.all_gather(message, 'rep', axis=0, tiled=True)  36.9 us
    mul x1, local copies, waits for them, and re-layouts, per_device(): dense * keeper[:, None, :, :, None]  27.8 us
    mul x1, other arithmetic, per_device(): dense * keeper[:, None, :, :, None]  19.8 us
    dot_general x1, matrix products, per_device(): jnp.dot(strip, lax.all_gather(own, 'row', axis=0, tiled=True), preferred_...  12.6 us
    dot_general x1, matrix products, per_device(): lax.dot_general(strip, lax.all_gather(message, 'rep', axis=0, tiled=True)...  12.3 us
  transfers between devices with their start and end apart: 5, of which 4 were waited for; matrix products, arithmetic and copies ran while one was open for 14% of the time, Pallas kernels for 0%

commit v1 on v0

--- a/solution.py
+++ b/solution.py
@@ -63,7 +63,9 @@
         lax.dot_general(mean, dpre_b, contract_first, preferred_element_type=jnp.float32) * scale
     )
     bias_term = jnp.sum(dpre, axis=0) * scale
-    grad_self, grad_neigh, grad_bias = lax.psum((self_term, neigh_term, bias_term), ("row", "rep"))
+    grad_self, grad_neigh, grad_bias = lax.psum(
+        lax.psum((self_term, neigh_term, bias_term), "row"), "rep"
+    )
     message = (
         lax.dot_general(dpre_b, neigh_weight, contract_second, preferred_element_type=jnp.float32)
         / degree

time: 430 us -> 476 us (1.11)
  waiting for transfers between devices: 255 us -> 313 us
  blocking collectives: 66 us -> 53.8 us
    psum x1 -> x2, waiting for transfers between devices: 151 us -> 190 us  [the longest x1 119 us: per_device(): lax.psum(lax.psum((self_term, neigh_term, bias_term), 'row'), 'rep')]
    reduce_scatter x1, waiting for transfers between devices: 1.76 us -> 23.4 us  [per_device(): lax.psum_scatter(partial_back.astype(jnp.bfloat16), 'row', scatter_dimens...]
    psum x1 -> x2, blocking collectives: 66 us -> 53.8 us  [the longest x1 36.2 us: per_device(): lax.psum(lax.psum((self_term, neigh_term, bias_term), 'row'), 'rep')]
  transfers between devices with their start and end apart: 5 -> 6, of which waited for: 4 -> 5; matrix products, arithmetic and copies ran while one was open for 14% -> 15% of each run, Pallas kernels for 0% -> 0%
where the time goes in v1:
time: 476 us; the launch traced here: 475 us
  waiting for transfers between devices  313 us (66%)
  blocking collectives  53.8 us (11%)
  local copies, waits for them, and re-layouts  34.2 us (7%)
  matrix products  32.7 us (7%)
  other arithmetic  27 us (6%)
  between operations  14.2 us (3%)
    psum x1, waiting for transfers between devices, per_device(): lax.psum(lax.psum((self_term, neigh_term, bias_term), 'row'), 'rep')  119 us
    psum x1, waiting for transfers between devices, per_device(): lax.psum((self_term, neigh_term, bias_term), 'row')  70.4 us
    reduce_scatter x1, waiting for transfers between devices, per_device(): lax.psum_scatter(partial_sums, 'rep', scatter_dimension=0, tiled=True)  66 us
    psum x1, blocking collectives, per_device(): lax.psum(lax.psum((self_term, neigh_term, bias_term), 'row'), 'rep')  36.2 us
    all_gather x1, waiting for transfers between devices, per_device(): lax.all_gather(message, 'rep', axis=0, tiled=True)  33.9 us
    mul x1, local copies, waits for them, and re-layouts, per_device(): dense * keeper[:, None, :, :, None]  27.7 us
    reduce_scatter x1, waiting for transfers between devices, per_device(): lax.psum_scatter(partial_back.astype(jnp.bfloat16), 'row', scatter_dimens...  23.4 us
    mul x1, other arithmetic, per_device(): dense * keeper[:, None, :, :, None]  19.8 us
  transfers between devices with their start and end apart: 6, of which 5 were waited for; matrix products, arithmetic and copies ran while one was open for 15% of the time, Pallas kernels for 0%

profile of v1, /device:TPU:1, one launch (start us, length us, event | category | flops | bytes accessed | tf_op | source)
XLA Modules:
  0.0 475.3 jit_solution(5848590697566996618)
XLA Ops:
  7.2 1.5 copy-done
  8.8 0.7 constant_dynamic-slice_fusion
  9.5 0.8 copy.14
  10.3 0.7 broadcast_compare_fusion
  11.1 6.3 %convert_element_type.45 = bf16[4096,8,128]{2,1,0:T(8,128)(2,1)S(1)} convert(s32[4096,8,128]{2,1,0:T(8,128)} %param.13) | non-fusion elementwise | flops 4194304 | bytes 25165824 | tf_op jit(solution)/shard_map/convert_element_type | solution.py:37
  17.5 19.8 %broadcast_multiply_fusion = bf16[32,128,8,2,128]{4,3,2,1,0:T(2,128)(2,1)} fusion(bf16[32,8,2]{2,1,0:T(8,128)(2,1)S(1)} %fusion.13, bf16[32,128,8,128]{3,2,1,0:T(8,128)(2,1)S(1)} %bitcast.15), kind=kLoop, calls=%fused_computation | loop fusion | flops 8388608 | bytes 25166848 | tf_op jit(solution)/shard_map/mul | solution.py:40
  37.3 27.7 %mul.80 = bf16[4096,2048]{1,0:T(8,128)(2,1)} reshape(bf16[32,128,8,2,128]{4,3,2,1,0:T(2,128)(2,1)} %broadcast_multiply_fusion) | data formatting | bytes 33554432 | tf_op jit(solution)/shard_map/mul | solution.py:40
  65.1 12.6 %fusion.17 = f32[4096,256]{1,0:T(8,128)} fusion(bf16[4096,2048]{1,0:T(8,128)(2,1)} %mul.80, bf16[2048,256]{1,0:T(8,128)(2,1)} %all-gather.3.cloned.1.call-done), kind=kOutput, calls=%fused_computation.33 | convolution fusion | flops 4294967296 | bytes 22020096 | tf_op jit(solution)/shard_map/dot_general | solution.py:43
  78.1 66.0 %reduce-scatter.3.cloned.1.call-done = f32[256,256]{1,0:T(8,128)} async-done(((f32[4096,256]{1,0:T(8,128)}), f32[256,256]{1,0:T(8,128)}) %reduce-scatter.3.cloned.1.call-update) | async-done | bytes 262160 | tf_op jit(solution)/shard_map/reduce_scatter | solution.py:46
  144.1 2.0 fusion.14
  146.1 0.9 fusion.2
  147.1 0.9 convolution_multiply_fusion.1
  148.0 2.0 convolution_multiply_fusion
  150.0 0.2 reduce-scatter.5.cloned.1.call-start
  150.2 33.9 %all-gather.5.cloned.1.call-done = bf16[4096,256]{1,0:T(8,128)(2,1)} async-done(((bf16[256,256]{1,0:T(8,128)(2,1)}), bf16[4096,256]{1,0:T(8,128)(2,1)}) %all-gather.5.cloned.1.call-update) | async-done | bytes 2097168 | tf_op jit(solution)/shard_map/all_gather | solution.py:79
  184.1 12.3 %convolution_convert_fusion = bf16[2048,256]{1,0:T(8,128)(2,1)} fusion(bf16[4096,2048]{1,0:T(8,128)(2,1)} %mul.80, bf16[4096,256]{1,0:T(8,128)(2,1)} %all-gather.5.cloned.1.call-done), kind=kOutput, calls=%fused_computation.1 | convolution fusion | flops 4295491584 | bytes 19922944 | tf_op jit(solution)/shard_map/dot_general | solution.py:77
  196.5 70.4 %all-reduce.7.cloned.1.call-done = (f32[256,256]{1,0:T(8,128)}, f32[256,256]{1,0:T(8,128)}) async-done(((f32[256,256]{1,0:T(8,128)}, f32[256,256]{1,0:T(8,128)}), (f32[256,256]{1,0:T(8,128)}, f32[256,256]{1,0:T(8,128)})) %all-reduce.7.cloned.1.call-update) | async-done | bytes 524304 | tf_op jit(solution)/shard_map/psum | solution.py:67
  266.9 17.5 %psum.46 = f32[256]{0:T(256)S(1)} all-reduce(f32[256]{0:T(256)S(1)} %broadcast_multiply_fusion.1), channel_id=1, replica_groups=mesh['row'=8,'rep'=16] {'row'}, use_global_device_ids=true, to_apply=%region_7.0 | all-reduce | flops 256 | bytes 2048 | tf_op jit(solution)/shard_map/psum | solution.py:67
  284.4 36.2 %psum.47 = f32[256]{0:T(256)} all-reduce(f32[256]{0:T(256)S(1)} %psum.46), channel_id=1, replica_groups=mesh['row'=8,'rep'=16] {'rep'}, use_global_device_ids=true, to_apply=%region_8.0 | all-reduce | flops 256 | bytes 2048 | tf_op jit(solution)/shard_map/psum | solution.py:66
  320.7 23.4 %reduce-scatter.5.cloned.1.call-done = bf16[256,256]{1,0:T(8,128)(2,1)} async-done(((bf16[2048,256]{1,0:T(8,128)(2,1)}), bf16[256,256]{1,0:T(8,128)(2,1)}) %reduce-scatter.5.cloned.1.call-update) | async-done | bytes 131088 | tf_op jit(solution)/shard_map/reduce_scatter | solution.py:83
  344.1 1.8 fusion.1
  345.9 119.3 %all-reduce.5.cloned.1.call-done = (f32[256,256]{1,0:T(8,128)}, f32[256,256]{1,0:T(8,128)}) async-done(((f32[256,256]{1,0:T(8,128)}, f32[256,256]{1,0:T(8,128)}), (f32[256,256]{1,0:T(8,128)}, f32[256,256]{1,0:T(8,128)})) %all-reduce.5.cloned.1.call-update) | async-done | bytes 524304 | tf_op jit(solution)/shard_map/psum | solution.py:66
  465.1 1.7 copy.20
  466.8 1.7 copy.21
  (32 shorter events, 0.8 us)
Async XLA Ops:
  7.2 1.6 copy-start
  7.2 58.0 %all-gather.3.cloned.1.call-start = ((), (), s32[]{:S(2)}) async-start(), calls=%async_computation.2 | async-start | bytes 1179648 | tf_op jit(solution)/shard_map/all_gather | solution.py:44
  9.5 134.6 %reduce-scatter.3.cloned.1.call-start = ((), (), s32[]{:S(2)}) async-start(), calls=%async_computation.3 | async-start | bytes 4456448 | tf_op jit(solution)/shard_map/reduce_scatter | solution.py:46
  65.1 12.7 %copy-start.4 = (s32[256]{0:T(256)S(1)}, s32[256]{0:T(256)}, u32[]{:S(2)}) copy-start(s32[256]{0:T(256)} %param.16) | copy-start | bytes 3076
  65.1 12.8 %copy-start.2 = (bf16[256,256]{1,0:T(8,128)(2,1)S(1)}, bf16[256,256]{1,0:T(8,128)(2,1)}, u32[]{:S(2)}) copy-start(bf16[256,256]{1,0:T(8,128)(2,1)} %constant_dynamic-slice_fusion) | copy-start | bytes 393220
  65.1 12.8 %copy-start.3 = (bf16[256,256]{1,0:T(8,128)(2,1)S(1)}, bf16[256,256]{1,0:T(8,128)(2,1)}, u32[]{:S(2)}) copy-start(bf16[256,256]{1,0:T(8,128)(2,1)} %param.10) | copy-start | bytes 393220
  65.1 79.0 %copy-start.5 = (bf16[256,256]{1,0:T(8,128)(2,1)S(1)}, bf16[256,256]{1,0:T(8,128)(2,1)}, u32[]{:S(2)}) copy-start(bf16[256,256]{1,0:T(8,128)(2,1)} %param.17) | copy-start | bytes 393220
  65.1 79.0 %copy-start.6 = (bf16[256,256]{1,0:T(8,128)(2,1)S(1)}, bf16[256,256]{1,0:T(8,128)(2,1)}, u32[]{:S(2)}) copy-start(bf16[256,256]{1,0:T(8,128)(2,1)} %param.11) | copy-start | bytes 393220
  65.1 79.0 %copy-start.7 = (f32[256]{0:T(256)S(1)}, f32[256]{0:T(256)}, u32[]{:S(2)}) copy-start(f32[256]{0:T(256)} %param.12) | copy-start | bytes 3076
  77.8 106.3 %all-gather.5.cloned.1.call-start = ((), (), s32[]{:S(2)}) async-start(), calls=%async_computation.4 | async-start | bytes 2228224 | tf_op jit(solution)/shard_map/all_gather | solution.py:79
  147.0 119.8 %all-reduce.7.cloned.1.call-start = ((), (), s32[]{:S(2)}) async-start(), calls=%async_computation.7 | async-start | bytes 1048576 | tf_op jit(solution)/shard_map/psum | solution.py:67
  150.0 318.5 %copy-start.1 = (bf16[4096,256]{1,0:T(8,128)(2,1)S(1)}, bf16[4096,256]{1,0:T(8,128)(2,1)}, u32[]{:S(2)}) copy-start(bf16[4096,256]{1,0:T(8,128)(2,1)} %param.9) | copy-start | bytes 6291460
  150.0 194.1 %reduce-scatter.5.cloned.1.call-start = ((), (), s32[]{:S(2)}) async-start(), calls=%async_computation.5 | async-start | bytes 1179648 | tf_op jit(solution)/shard_map/reduce_scatter | solution.py:83
  196.4 268.7 %all-reduce.5.cloned.1.call-start = ((), (), s32[]{:S(2)}) async-start(), calls=%async_computation.6 | async-start | bytes 1048576 | tf_op jit(solution)/shard_map/psum | solution.py:66
Sparse Core Ops, SparseCore 0:
  11.0 48.4 all-gather.2
  77.9 66.1 reduce-scatter.2
  147.1 36.9 all-gather.4
  187.1 79.7 all-reduce.6
  270.7 73.2 reduce-scatter.4
  346.4 118.6 all-reduce.4
